TPU v7x, 256 devices: a whole 4x4x8 slice. The times are simulated.
256 devices in a mesh: tm: 8 (over z), row: 8 (over x, core), obs: 4 (over y).
Axes of the slice: x: 4, y: 4, z: 8, core: 2. Of those that a mesh axis runs over, the one named last changes fastest.
Arguments:
- dyn_pattern: int32 [16, 8, 3], P('tm'), may hold values from 0 to 7
- dyn_values: float32 [16, 1024, 384], P('tm', ('row', 'obs')), may hold values from -0.3125 to 0.3125
- offsets: float32 [16, 1024], P('tm', ('row', 'obs')), may hold values from -6 to 6
- covariance: float32 [16, 1024, 1024], P('tm', ('row', 'obs')), may hold values from -1 to 14, as said below
- obs_block: int32 [16, 128], P('tm'), may hold values from 0 to 7
- obs_matrix: float32 [16, 128, 256], P('tm', 'obs'), may hold values from -0.375 to 0.375
- obs_data: float32 [16, 128], P('tm', 'obs'), may hold values from -6 to 6
Outputs:
- scan_dynamics: float32 [8, 1024, 1024], P('tm', ('row', 'obs'))
- scan_offset: float32 [8, 1024], P('tm', ('row', 'obs'))
- scan_covariance: float32 [8, 1024, 1024], P('tm', ('row', 'obs'))
- scan_factor: float32 [8, 1024, 512], P('tm', ('row', 'obs'))
- scan_information: float32 [8, 1024], P('tm', ('row', 'obs'))
Inputs may be any that keep to these rules, and one draw needn't show every extreme that they name: `dyn_pattern`: each entry names a block column. `obs_block`: each entry names a state block. Each covariance is symmetric and positive definite.
All inputs are finite; a program needn't handle non-finite values.
Results may differ from a plain program's by a relative error of at most 0.00019.
Values sent between devices are 32-bit elements; how exact they have to be, the bound alone decides.
A program may use at most 128 MiB of HBM per device.

v0:
```python
import jax
import jax.numpy as jnp
from jax import lax
from jax.sharding import PartitionSpec as P

largest_value = lax.Precision.HIGHEST


def shifted(block, axis, distance):
    devices = range(lax.axis_size(axis))
    route = [(i - distance, i) for i in devices if i - distance in devices]
    return lax.ppermute(block, axis, route)


def product(left, right):
    return jnp.dot(left, right, precision=largest_value, preferred_element_type=jnp.float32)


def lower_solve(lower, rhs):
    return lax.linalg.triangular_solve(lower, rhs, left_side=True, lower=True)


def assemble_dynamics(pattern, values):
    number_of_blocks = pattern.shape[0]
    per_row = pattern.shape[1]
    states = values.shape[0]
    block_extent = states // number_of_blocks
    indicator_matrix = (
        pattern[:, :, None] == jnp.arange(number_of_blocks, dtype=jnp.int32)[None, None, :]
    ).astype(jnp.float32)
    blocks = values.reshape(number_of_blocks, block_extent, per_row, block_extent)
    return jnp.einsum("ckd,cikj->cidj", indicator_matrix, blocks, precision=largest_value).reshape(
        states, states
    )


def assemble_factor(indices, matrix, number_of_blocks):
    item_count = matrix.shape[0]
    block_extent = matrix.shape[1] // 2
    reach = (indices[:, None] + jnp.arange(2, dtype=jnp.int32)[None, :]) % number_of_blocks
    indicator_matrix = (
        reach[:, :, None] == jnp.arange(number_of_blocks, dtype=jnp.int32)[None, None, :]
    ).astype(jnp.float32)
    piece_list = matrix.reshape(item_count, 2, block_extent)
    return jnp.einsum(
        "onr,onz->rzo", indicator_matrix, piece_list, precision=largest_value
    ).reshape(number_of_blocks * block_extent, item_count)


def combine(
    prior_dyn,
    prior_offsets,
    prior_cov,
    prior_factor,
    prior_zeta,
    own_dyn,
    own_offsets,
    own_cov,
    own_factor,
    own_zeta,
    row_start,
):
    panel_rows = prior_cov.shape[0]
    rank_width = own_factor.shape[1]
    own_pan = lax.dynamic_slice_in_dim(own_dyn, row_start, panel_rows, 0)
    gain_pan = product(prior_cov, own_factor)
    gain_rows = lax.all_gather(gain_pan, ("row", "obs"), axis=0, tiled=True)
    identity = jnp.eye(rank_width, dtype=jnp.float32)
    factor_pan = lax.dynamic_slice_in_dim(own_factor, row_start, panel_rows, 0)
    system = identity + lax.psum(product(factor_pan.T, gain_pan), ("row", "obs"))
    lower = jnp.linalg.cholesky(system)
    carried = product(own_dyn, gain_rows)
    observed = product(prior_dyn.T, own_factor)
    upper_part = lower_solve(lower, observed.T)
    weights = lower_solve(lower, carried.T).T
    weight_pan = lax.dynamic_slice_in_dim(weights, row_start, panel_rows, 0)
    spread_pan = product(prior_cov, own_dyn.T)
    moved = product(own_pan, lax.all_gather(spread_pan, ("row", "obs"), axis=0, tiled=True))
    new_dyn = product(own_pan, prior_dyn) - product(weight_pan, upper_part)
    new_cov = moved - product(weight_pan, weights.T) + own_cov
    residual = own_zeta - product(own_factor.T, prior_offsets)
    solved = lower_solve(lower, residual[:, None])[:, 0]
    new_offsets = product(own_pan, prior_offsets) + product(weight_pan, solved) + own_offsets
    upper_pan = lax.dynamic_slice_in_dim(upper_part, row_start, panel_rows, 1).T
    new_factor = jnp.concatenate([upper_pan, prior_factor], axis=1)
    new_zeta = jnp.concatenate([solved, prior_zeta])
    return (new_dyn, new_offsets, new_cov, new_factor, new_zeta)


def per_device(dyn_pattern, dyn_values, offsets, covariance, obs_block, obs_matrix, obs_data):
    panel_rows = covariance.shape[1]
    row_start = lax.axis_index(("row", "obs")) * panel_rows
    number_of_blocks = dyn_pattern.shape[1]
    obs_rows, obs_values = (
        lax.all_gather(obs_matrix, "obs", axis=1, tiled=True),
        lax.all_gather(obs_data, "obs", axis=1, tiled=True),
    )
    row_values, row_offsets = (
        lax.all_gather(dyn_values, ("row", "obs"), axis=1, tiled=True),
        lax.all_gather(offsets, ("row", "obs"), axis=1, tiled=True),
    )
    first_dyn = assemble_dynamics(dyn_pattern[0], row_values[0])
    second_dyn = assemble_dynamics(dyn_pattern[1], row_values[1])
    first_factor = assemble_factor(obs_block[0], obs_rows[0], number_of_blocks)
    second_factor = assemble_factor(obs_block[1], obs_rows[1], number_of_blocks)
    first_pan = lax.dynamic_slice_in_dim(first_factor, row_start, panel_rows, 0)
    dyn_pan, off_pan, cov_pan, fac_pan, zeta_full = combine(
        first_dyn,
        row_offsets[0],
        covariance[0],
        first_pan,
        obs_values[0],
        second_dyn,
        offsets[1],
        covariance[1],
        second_factor,
        obs_values[1],
        row_start,
    )
    later_pan, later_cov, later_off, later_fac, later_zeta = shifted(
        (dyn_pan, cov_pan, off_pan, fac_pan, zeta_full), "tm", -1
    )
    prior_full, later_full, later_factor, prior_offsets = (
        lax.all_gather(dyn_pan, ("row", "obs"), axis=0, tiled=True),
        lax.all_gather(later_pan, ("row", "obs"), axis=0, tiled=True),
        lax.all_gather(later_fac, ("row", "obs"), axis=0, tiled=True),
        lax.all_gather(off_pan, ("row", "obs"), axis=0, tiled=True),
    )
    top_dyn, top_off, top_cov, top_fac, top_zeta = combine(
        prior_full,
        prior_offsets,
        cov_pan,
        fac_pan,
        zeta_full,
        later_full,
        later_off,
        later_cov,
        later_factor,
        later_zeta,
        row_start,
    )
    even_turn = lax.axis_index("tm") % 2 == 0
    padded_fac = jnp.concatenate([fac_pan, jnp.zeros_like(fac_pan)], axis=1)
    padded_zeta = jnp.concatenate([zeta_full, jnp.zeros_like(zeta_full)])
    out_dyn = jnp.where(even_turn, top_dyn, dyn_pan)
    out_off = jnp.where(even_turn, top_off, off_pan)
    out_cov = jnp.where(even_turn, top_cov, cov_pan)
    out_fac = jnp.where(even_turn, top_fac, padded_fac)
    out_zeta = jnp.where(even_turn, top_zeta, padded_zeta)
    output_information = product(out_fac, out_zeta)
    return (out_dyn[None], out_off[None], out_cov[None], out_fac[None], output_information[None])


def solution(mesh):
    placed = (
        P("tm", None, None),
        P("tm", ("row", "obs"), None),
        P("tm", ("row", "obs")),
        P("tm", ("row", "obs"), None),
        P("tm", None),
        P("tm", "obs", None),
        P("tm", "obs"),
    )
    return jax.shard_map(
        per_device,
        mesh=mesh,
        in_specs=placed,
        out_specs=(
            P("tm", ("row", "obs"), None),
            P("tm", ("row", "obs")),
            P("tm", ("row", "obs"), None),
            P("tm", ("row", "obs"), None),
            P("tm", ("row", "obs")),
        ),
        check_vma=False,
    )
```

profile of v0, /device:TPU:1, one launch (start us, length us, event | category | flops | bytes accessed | tf_op | source)
XLA Modules:
  0.0 616.6 jit_solution(8064863237237655006)
XLA Ops:
  7.2 0.7 all-gather.10.cloned.1.call-update
  8.0 11.5 %all_gather.37 = f32[2,128,256]{2,1,0:T(8,128)S(1)} all-gather(f32[2,32,256]{2,1,0:T(8,128)} %param.16), channel_id=1, replica_groups=mesh['tm'=8,'row'=8,'obs'=4] {'obs'}, dimensions={1}, use_global_device_ids=true | all-gather | bytes 327680 | tf_op jit(solution)/shard_map/all_gather | solution.py:95
  19.5 0.8 slice_bitcast_fusion.12
  20.4 0.9 fusion.36
  21.4 1.5 fusion.42
  23.0 0.9 fusion.83
  24.0 40.9 %all-gather.10.cloned.1.call-done = f32[2,1024,384]{2,1,0:T(8,128)} async-done(((f32[2,32,384]{2,1,0:T(8,128)}), f32[2,1024,384]{2,1,0:T(8,128)}) %all-gather.10.cloned.1.call-update) | async-done | bytes 3145744 | tf_op jit(solution)/shard_map/all_gather | solution.py:99
  64.9 3.2 fusion.135
  68.2 3.6 reshape.312
  71.8 4.3 fusion.104
  76.1 2.0 copy-done
  78.1 4.9 convolution_bitcast_fusion.1
  83.5 0.9 convolution_bitcast_fusion
  84.7 89.2 %all-reduce.5.cloned.1.call-done = f32[128,128]{1,0:T(8,128)} async-done(((f32[128,128]{1,0:T(8,128)}), f32[128,128]{1,0:T(8,128)}) %all-reduce.5.cloned.1.call-update) | async-done | bytes 65552 | tf_op jit(solution)/shard_map/psum | solution.py:70
  173.8 0.9 convert_add_fusion.1
  174.8 0.9 fusion.77
  175.6 11.7 %cholesky.60 = f32[128,128]{1,0:T(8,128)S(1)} custom-call(f32[128,128]{1,0:T(8,128)S(1)} %fusion.77), custom_call_target="Cholesky" | custom-call | tf_op jit(solution)/shard_map/jit(cholesky)/cholesky | solution.py:71
  188.0 0.7 fusion.55
  188.7 9.8 %custom-call.31 = f32[1,128,128]{1,2,0:T(8,128)S(1)} custom-call(f32[1,128,128]{2,1,0:T(8,128)S(1)} %fusion.55), custom_call_target="InvertDiagBlocksLowerTriangular" | custom-call | tf_op jit(solution)/shard_map/triangular_solve/custom-call.4 | solution.py:20
  198.5 2.2 reshape.313
  200.7 4.3 fusion.107
  205.1 2.0 copy-done.2
  207.1 3.0 fusion
  210.9 1.3 collective-permute-start.1
  212.1 3.8 collective-permute-done.1
  216.6 42.6 %all_gather.38 = f32[1024,128]{1,0:T(8,128)S(1)} all-gather(f32[32,128]{1,0:T(8,128)S(1)} %bitcast.273), channel_id=1, replica_groups=mesh['tm'=8,'row'=8,'obs'=4] {'row','obs'}, dimensions={0}, use_global_device_ids=true | all-gather | bytes 540672 | tf_op jit(solution)/shard_map/all_gather | solution.py:67
  259.2 3.4 copy.79
  262.6 4.8 fusion.133
  268.5 3.0 fusion.6
  271.5 1.4 collective-permute-start
  273.0 4.4 collective-permute-done
  277.4 0.7 copy-done.12
  278.9 4.8 fusion.52
  284.2 1.9 fusion.138
  286.1 1.9 fusion.100
  288.1 0.7 all-gather.20.cloned.1.call-update
  288.9 40.2 %all-gather = f32[32,32,2]{1,2,0:T(2,128)S(1)} all-gather(f32[1,32,2]{1,2,0:T(2,128)S(1)} %bitcast.282), channel_id=1, replica_groups=mesh['tm'=8,'row'=8,'obs'=4] {'row','obs'}, dimensions={0}, use_global_device_ids=true | all-gather | bytes 8448 | tf_op jit(solution)/shard_map/all_gather | solution.py:100
  329.1 5.2 all-gather.1
  334.5 0.7 fusion.175
  335.7 6.7 %fusion.141 = f32[32,1024]{1,0:T(8,128)} fusion(f32[32,1024]{1,0:T(8,128)S(1)} %fusion.12, f32[1024,1024]{1,0:T(8,128)} %all-gather.12.cloned.1.call-done), kind=kOutput, calls=%fused_computation.205 | convolution fusion | flops 402653184 | bytes 4456448 | tf_op jit(solution)/shard_map/dot_general | solution.py:16
  343.9 1.3 collective-permute-start.2
  345.3 1.1 convolution_bitcast_fusion.9
  346.6 1.3 collective-permute-start.3
  348.2 63.2 %all-reduce.1 = f32[1024]{0:T(1024)S(1)} all-reduce(f32[1024]{0:T(1024)S(1)} %dynamic-update-slice.17), channel_id=1, replica_groups=mesh['tm'=8,'row'=8,'obs'=4] {'row','obs'}, use_global_device_ids=true, to_apply=%add.1 | all-reduce | flops 1024 | bytes 8192
  412.1 1.3 collective-permute-start.4
  413.4 6.0 fusion.140
  419.4 80.5 %all-reduce.7.cloned.1.call-done = f32[256,256]{0,1:T(8,128)} async-done(((f32[256,256]{0,1:T(8,128)}), f32[256,256]{0,1:T(8,128)}) %all-reduce.7.cloned.1.call-update) | async-done | bytes 262160 | tf_op jit(solution)/shard_map/psum | solution.py:70
  499.9 1.0 convert_add_fusion
  501.0 1.0 fusion.34
  502.0 11.7 %cholesky.115 = f32[128,128]{1,0:T(8,128)S(1)} custom-call(f32[128,128]{1,0:T(8,128)S(1)} %cholesky.141), custom_call_target="Cholesky" | custom-call | tf_op jit(solution)/shard_map/jit(cholesky)/cholesky | solution.py:71
  513.8 9.8 %custom-call.26 = f32[1,128,128]{1,2,0:T(8,128)S(1)} custom-call(f32[1,128,128]{2,1,0:T(8,128)S(1)} %get-tuple-element.62), custom_call_target="InvertDiagBlocksLowerTriangular" | custom-call | tf_op jit(solution)/shard_map/jit(cholesky)/cholesky | solution.py:71
  524.1 11.7 %cholesky.128 = f32[128,128]{1,0:T(8,128)S(1)} custom-call(f32[128,128]{1,0:T(8,128)S(1)} %convolution_subtract_fusion.3), custom_call_target="Cholesky" | custom-call | tf_op jit(solution)/shard_map/jit(cholesky)/cholesky | solution.py:71
  538.5 4.0 while.5
  539.1 1.4 bitcast_dynamic-update-slice_fusion.2
  541.1 1.4 bitcast_dynamic-update-slice_fusion.2
  542.5 19.8 %custom-call.33 = f32[2,128,128]{1,2,0:T(8,128)S(1)} custom-call(f32[2,128,128]{2,1,0:T(8,128)S(1)} %get-tuple-element.29), custom_call_target="InvertDiagBlocksLowerTriangular" | custom-call | tf_op jit(solution)/shard_map/triangular_solve/custom-call.5 | solution.py:20
  565.1 0.7 fusion.60
  566.5 9.2 %fusion.139 = f32[256,1024]{1,0:T(8,128)S(1)} fusion(f32[1024,256]{1,0:T(8,128)} %all-gather.20.cloned.1.call-done, f32[1024,1024]{1,0:T(8,128)} %all-gather.12.cloned.1.call-done), kind=kOutput, calls=%fused_computation.203 | convolution fusion | flops 3221225472 | bytes 6291456 | tf_op jit(solution)/shard_map/dot_general | solution.py:16
  577.7 0.7 fusion.24
  578.4 0.7 fusion.23
  579.2 4.1 fusion.14
  583.4 1.7 fusion.20
  585.1 19.4 %all-gather.22.cloned.1.call-done = f32[1024,1024]{1,0:T(8,128)} async-done(((f32[32,1024]{1,0:T(8,128)}), f32[1024,1024]{1,0:T(8,128)}) %all-gather.22.cloned.1.call-update) | async-done | bytes 4194320 | tf_op jit(solution)/shard_map/all_gather | solution.py:78
  604.5 5.4 fusion.11
  (127 shorter events, 17.6 us)
Async XLA Ops:
  7.2 16.8 %copy-start.15 = (s32[2,8,3]{1,0,2:T(2,128)S(1)}, s32[2,8,3]{1,0,2:T(2,128)}, u32[]{:S(2)}) copy-start(s32[2,8,3]{1,0,2:T(2,128)} %param.11) | copy-start | bytes 580
  7.2 57.8 %all-gather.10.cloned.1.call-start = ((), (), s32[]{:S(2)}) async-start(), calls=%async_computation | async-start | bytes 3244032 | tf_op jit(solution)/shard_map/all_gather | solution.py:99
  7.9 165.9 %all-reduce.5.cloned.1.call-start = ((), (), s32[]{:S(2)}) async-start(), calls=%async_computation.1 | async-start | bytes 131072 | tf_op jit(solution)/shard_map/psum | solution.py:70
  23.9 255.0 %all-gather.18.cloned.1.call-start = ((), (), s32[]{:S(2)}) async-start(), calls=%async_computation.5 | async-start | bytes 4325376 | tf_op jit(solution)/shard_map/all_gather | solution.py:78
  68.2 9.9 %copy-start.10 = (f32[2,32,1024]{2,1,0:T(8,128)S(1)}, f32[2,32,1024]{2,1,0:T(8,128)}, u32[]{:S(2)}) copy-start(f32[2,32,1024]{2,1,0:T(8,128)} %param.14) | copy-start | bytes 786436
  76.1 2.0 copy-start
  83.0 201.2 %all-gather.16.cloned.1.call-start = ((), (), s32[]{:S(2)}) async-start(), calls=%async_computation.4 | async-start | bytes 1081344 | tf_op jit(solution)/shard_map/all_gather | solution.py:126
  84.6 120.4 %copy-start.9 = (f32[8,128,128]{2,1,0:T(8,128)}, f32[8,128,128]{2,1,0:T(8,128)S(1)}, u32[]{:S(2)}) copy-start(f32[8,128,128]{2,1,0:T(8,128)S(1)} %copy.56) | copy-start | bytes 1572868
  205.0 2.0 copy-start.2
  210.9 5.0 collective-permute-start.1
  215.9 0.6 copy-start.13
  216.5 119.2 %all-gather.12.cloned.1.call-start = ((), (), s32[]{:S(2)}) async-start(), calls=%async_computation.2 | async-start | bytes 4325376 | tf_op jit(solution)/shard_map/all_gather | solution.py:125
  259.2 3.5 copy-start.1
  262.6 5.9 copy-start.6
  262.6 5.9 copy-start.3
  271.5 6.6 %copy-start.7 = (f32[32,1024]{1,0:T(8,128)}, f32[32,1024]{1,0:T(8,128)S(1)}, u32[]{:S(2)}) copy-start(f32[32,1024]{1,0:T(8,128)S(1)} %fusion.6) | copy-start | bytes 393220
  271.5 17.3 %copy-start.14 = (f32[2,32]{1,0:T(2,128)S(1)}, f32[2,32]{1,0:T(2,128)}, u32[]{:S(2)}) copy-start(f32[2,32]{1,0:T(2,128)} %param.13) | copy-start | bytes 772
  271.5 57.6 %copy-start.16 = (f32[2,32]{1,0:T(2,128)S(1)}, f32[2,32]{1,0:T(2,128)}, u32[]{:S(2)}) copy-start(f32[2,32]{1,0:T(2,128)} %param.17) | copy-start | bytes 772
  271.5 5.8 collective-permute-start
  277.4 0.7 copy-start.12
  278.1 135.3 %all-gather.14.cloned.1.call-start = ((), (), s32[]{:S(2)}) async-start(), calls=%async_computation.3 | async-start | bytes 4325376 | tf_op jit(solution)/shard_map/all_gather | solution.py:124
  278.6 221.2 %all-reduce.7.cloned.1.call-start = ((), (), s32[]{:S(2)}) async-start(), calls=%async_computation.6 | async-start | bytes 524288 | tf_op jit(solution)/shard_map/psum | solution.py:70
  283.7 58.8 %copy-start.17 = (u32[256]{0:T(256)S(1)}, u32[256]{0:T(256)}, u32[]{:S(2)}) copy-start(u32[256]{0:T(256)} %constant.217) | copy-start | bytes 3076
  284.2 127.2 %copy-start.5 = (f32[1024,256]{1,0:T(8,128)S(1)}, f32[1024,256]{1,0:T(8,128)}, u32[]{:S(2)}) copy-start(f32[1024,256]{1,0:T(8,128)} %all-gather.16.cloned.1.call-done) | copy-start | bytes 3145732
  286.1 2.0 copy-start.11
  288.1 278.4 %all-gather.20.cloned.1.call-start = ((), (), s32[]{:S(2)}) async-start(), calls=%async_computation.7 | async-start | bytes 1081344 | tf_op jit(solution)/shard_map/all_gather | solution.py:67
  288.8 315.7 %all-gather.22.cloned.1.call-start = ((), (), s32[]{:S(2)}) async-start(), calls=%async_computation.8 | async-start | bytes 4325376 | tf_op jit(solution)/shard_map/all_gather | solution.py:78
  343.9 68.2 %collective-permute-start.2 = (f32[256]{0:T(256)S(1)}, f32[256]{0:T(256)S(1)}, u32[]{:S(2)}, u32[]{:S(2)}) collective-permute-start(f32[256]{0:T(256)S(1)} %pad_maximum_fusion.5), channel_id=1, source_target_pairs={{32,0},{64,32},{96,64},{128,96},{160,128},{192,160},{224,192},{33,... | collective-permute-start | bytes 3080 | tf_op jit(solution)/shard_map/ppermute | solution.py:12
  346.6 236.8 %collective-permute-start.3 = (f32[32]{0:T(128)S(1)}, f32[32]{0:T(128)S(1)}, u32[]{:S(2)}, u32[]{:S(2)}) collective-permute-start(f32[32]{0:T(128)S(1)} %fusion.16), channel_id=1, source_target_pairs={{32,0},{64,32},{96,64},{128,96},{160,128},{192,160},{224,192},{33,... | collective-permute-start | bytes 392 | tf_op jit(solution)/shard_map/ppermute | solution.py:12
  412.1 173.0 %collective-permute-start.4 = (f32[32,1024]{1,0:T(8,128)S(1)}, f32[32,1024]{1,0:T(8,128)S(1)}, u32[]{:S(2)}, u32[]{:S(2)}) collective-permute-start(f32[32,1024]{1,0:T(8,128)S(1)} %fusion.12), channel_id=1, source_target_pairs={{32,0},{64,32},{96,64},{128,96},{160,128},{192,160},{224,192},{33,... | collective-permute-start | bytes 393224 | tf_op jit(solution)/shard_map/ppermute | solution.py:12
  575.7 3.5 copy-start.4
  575.7 3.5 copy-start.8
Sparse Core Ops, SparseCore 0:
  10.6 54.3 all-gather.9
  68.8 104.9 all-reduce.4
  177.3 50.7 all-gather.17
  231.4 47.2 all-gather.15
  281.4 50.4 all-gather.11
  335.2 50.5 all-gather.13
  389.4 110.4 all-reduce.6
  503.0 48.6 all-gather.19
  554.3 50.1 all-gather.21
where the time goes:
time: 624 us; the launch traced here: 617 us
  waiting for transfers between devices  240 us (38%)
  blocking collectives  163 us (26%)
  other arithmetic  82 us (13%)
  matrix products  81.8 us (13%)
  local copies, waits for them, and re-layouts  25.7 us (4%)
  between operations  16.7 us (3%)
  starting transfers between devices  7.45 us (1%)
    psum x2, waiting for transfers between devices, combine(): lax.psum(product(factor_pan.T, gain_pan), ('row', 'obs'))  170 us
    dot_general x25, matrix products, product(): jnp.dot(left, right, precision=largest_value, preferred_element_type=jnp....  65.3 us
    unnamed x1, blocking collectives  63.2 us
    another operation x10, other arithmetic, combine(): lower = jnp.linalg.cholesky(system)  47 us
    all_gather x1, blocking collectives, combine(): gain_rows = lax.all_gather(gain_pan, ('row', 'obs'), axis=0, tiled=True)  42.6 us
    all_gather x1, waiting for transfers between devices, per_device(): lax.all_gather(dyn_values, ('row', 'obs'), axis=1, tiled=True)  40.9 us
    all_gather x1, blocking collectives, per_device(): lax.all_gather(offsets, ('row', 'obs'), axis=1, tiled=True)  40.2 us
    another operation x8, other arithmetic, lower_solve(): return lax.linalg.triangular_solve(lower, rhs, left_side=True, lower=True)  30.5 us
  transfers between devices with their start and end apart: 14, of which 6 were waited for; matrix products, arithmetic and copies ran while one was open for 29% of the time, Pallas kernels for 0%

commit v1 on v0

--- a/solution.py
+++ b/solution.py
@@ -75,7 +75,15 @@
     weights = lower_solve(lower, carried.T).T
     weight_pan = lax.dynamic_slice_in_dim(weights, row_start, panel_rows, 0)
     spread_pan = product(prior_cov, own_dyn.T)
-    moved = product(own_pan, lax.all_gather(spread_pan, ("row", "obs"), axis=0, tiled=True))
+    moved = product(
+        own_pan,
+        jnp.concatenate(
+            lax.all_to_all(
+                jnp.stack([spread_pan] * lax.axis_size(("row", "obs"))), ("row", "obs"), 0, 0
+            ),
+            axis=0,
+        ),
+    )
     new_dyn = product(own_pan, prior_dyn) - product(weight_pan, upper_part)
     new_cov = moved - product(weight_pan, weights.T) + own_cov
     residual = own_zeta - product(own_factor.T, prior_offsets)

time: 624 us -> 682 us (1.093)
  waiting for transfers between devices: 240 us -> 280 us
  starting transfers between devices: 7.45 us -> 22.6 us
    all_gather x1, waiting for transfers between devices: 0.02 us -> 60.2 us  [per_device(): lax.all_gather(dyn_pan, ('row', 'obs'), axis=0, tiled=True)]
    all_gather x1, waiting for transfers between devices: 0.01 us -> 44.2 us  [combine(): gain_rows = lax.all_gather(gain_pan, ('row', 'obs'), axis=0, tiled=True)]
    psum x2, waiting for transfers between devices: 170 us -> 131 us  [combine(): lax.psum(product(factor_pan.T, gain_pan), ('row', 'obs'))]
    all_gather x2 -> x0, waiting for transfers between devices: 19.4 us -> none  [combine(): lax.all_gather(spread_pan, ('row', 'obs'), axis=0, tiled=True)]
    all_to_all x0 -> x2, starting transfers between devices: none -> 15 us  [combine(): lax.all_to_all(jnp.stack([spread_pan] * lax.axis_size(('row', 'obs'))), (...]
  transfers between devices with their start and end apart: 14 -> 14, of which waited for: 6 -> 5; matrix products, arithmetic and copies ran while one was open for 29% -> 24% of each run, Pallas kernels for 0% -> 0%
where the time goes in v1:
time: 682 us; the launch traced here: 674 us
  waiting for transfers between devices  280 us (41%)
  blocking collectives  162 us (24%)
  other arithmetic  81.9 us (12%)
  matrix products  78.2 us (11%)
  local copies, waits for them, and re-layouts  31.5 us (5%)
  starting transfers between devices  22.6 us (3%)
  between operations  17.1 us (3%)
    psum x2, waiting for transfers between devices, combine(): lax.psum(product(factor_pan.T, gain_pan), ('row', 'obs'))  131 us
    dot_general x25, matrix products, product(): jnp.dot(left, right, precision=largest_value, preferred_element_type=jnp....  64.8 us
    unnamed x1, blocking collectives  63.1 us
    all_gather x1, waiting for transfers between devices, per_device(): lax.all_gather(dyn_pan, ('row', 'obs'), axis=0, tiled=True)  60.2 us
    another operation x10, other arithmetic, combine(): lower = jnp.linalg.cholesky(system)  47 us
    all_gather x1, waiting for transfers between devices, combine(): gain_rows = lax.all_gather(gain_pan, ('row', 'obs'), axis=0, tiled=True)  44.2 us
    all_gather x1, blocking collectives, combine(): gain_rows = lax.all_gather(gain_pan, ('row', 'obs'), axis=0, tiled=True)  42.5 us
    all_gather x1, waiting for transfers between devices, per_device(): lax.all_gather(dyn_values, ('row', 'obs'), axis=1, tiled=True)  40.5 us
  transfers between devices with their start and end apart: 14, of which 5 were waited for; matrix products, arithmetic and copies ran while one was open for 24% of the time, Pallas kernels for 0%

profile of v1, /device:TPU:1, one launch (start us, length us, event | category | flops | bytes accessed | tf_op | source)
XLA Modules:
  0.0 674.2 jit_solution(15854060893253866422)
XLA Ops:
  7.9 11.5 %all_gather.31 = f32[2,128,256]{2,1,0:T(8,128)S(1)} all-gather(f32[2,32,256]{2,1,0:T(8,128)} %param.16), channel_id=1, replica_groups=mesh['tm'=8,'row'=8,'obs'=4] {'obs'}, dimensions={1}, use_global_device_ids=true | all-gather | bytes 327680 | tf_op jit(solution)/shard_map/all_gather | solution.py:103
  20.1 0.8 slice_bitcast_fusion.12
  21.0 0.9 fusion.36
  22.0 0.8 fusion.137
  22.9 1.5 fusion.42
  24.4 40.5 %all-gather.8.cloned.1.call-done = f32[2,1024,384]{2,1,0:T(8,128)} async-done(((f32[2,32,384]{2,1,0:T(8,128)}), f32[2,1024,384]{2,1,0:T(8,128)}) %all-gather.8.cloned.1.call-update) | async-done | bytes 3145744 | tf_op jit(solution)/shard_map/all_gather | solution.py:107
  64.9 3.7 fusion.135
  68.6 2.5 reshape.324
  71.2 2.7 fusion.104
  73.9 2.0 copy-done
  75.9 4.2 convolution_bitcast_fusion.1
  80.1 2.6 stack.4
  82.7 5.4 all-to-all-start
  88.2 0.9 fusion.83
  89.5 0.9 convolution_bitcast_fusion
  90.8 130.7 %all-reduce.5.cloned.1.call-done = f32[128,128]{1,0:T(8,128)} async-done(((f32[128,128]{1,0:T(8,128)}), f32[128,128]{1,0:T(8,128)}) %all-reduce.5.cloned.1.call-update) | async-done | bytes 65552 | tf_op jit(solution)/shard_map/psum | solution.py:70
  221.5 0.9 convert_add_fusion.1
  222.4 0.9 fusion.77
  223.3 11.7 %cholesky.60 = f32[128,128]{1,0:T(8,128)S(1)} custom-call(f32[128,128]{1,0:T(8,128)S(1)} %fusion.77), custom_call_target="Cholesky" | custom-call | tf_op jit(solution)/shard_map/jit(cholesky)/cholesky | solution.py:71
  236.3 9.8 %custom-call.31 = f32[1,128,128]{1,2,0:T(8,128)S(1)} custom-call(f32[1,128,128]{2,1,0:T(8,128)S(1)} %fusion.55), custom_call_target="InvertDiagBlocksLowerTriangular" | custom-call | tf_op jit(solution)/shard_map/triangular_solve/custom-call.4 | solution.py:20
  246.2 3.0 reshape.325
  249.2 2.7 fusion.107
  251.9 1.9 copy-done.2
  253.8 3.0 fusion
  257.6 1.3 collective-permute-start.1
  258.9 3.4 collective-permute-done.1
  263.0 42.5 %all_gather.32 = f32[1024,128]{1,0:T(8,128)S(1)} all-gather(f32[32,128]{1,0:T(8,128)S(1)} %bitcast.275), channel_id=1, replica_groups=mesh['tm'=8,'row'=8,'obs'=4] {'row','obs'}, dimensions={0}, use_global_device_ids=true | all-gather | bytes 540672 | tf_op jit(solution)/shard_map/all_gather | solution.py:67
  305.5 3.4 copy.79
  309.0 4.8 fusion.133
  314.9 3.0 fusion.6
  317.9 1.6 collective-permute-start
  319.6 4.8 fusion.52
  324.8 1.8 fusion.138
  326.7 1.9 fusion.100
  330.0 39.8 %all-gather = f32[32,32,2]{1,2,0:T(2,128)S(1)} all-gather(f32[1,32,2]{1,2,0:T(2,128)S(1)} %bitcast.284), channel_id=1, replica_groups=mesh['tm'=8,'row'=8,'obs'=4] {'row','obs'}, dimensions={0}, use_global_device_ids=true | all-gather | bytes 8448 | tf_op jit(solution)/shard_map/all_gather | solution.py:108
  369.9 5.2 all-gather.1
  377.2 1.3 collective-permute-start.2
  378.5 1.1 convolution_bitcast_fusion.9
  379.9 1.3 collective-permute-start.3
  381.5 63.1 %all-reduce.1 = f32[1024]{0:T(1024)S(1)} all-reduce(f32[1024]{0:T(1024)S(1)} %dynamic-update-slice.17), channel_id=1, replica_groups=mesh['tm'=8,'row'=8,'obs'=4] {'row','obs'}, use_global_device_ids=true, to_apply=%add.1 | all-reduce | flops 1024 | bytes 8192
  444.6 1.8 fusion.25
  446.4 1.5 collective-permute-start.4
  448.1 1.0 convert_add_fusion
  449.2 1.0 fusion.34
  450.2 11.7 %cholesky.115 = f32[128,128]{1,0:T(8,128)S(1)} custom-call(f32[128,128]{1,0:T(8,128)S(1)} %cholesky.141), custom_call_target="Cholesky" | custom-call | tf_op jit(solution)/shard_map/jit(cholesky)/cholesky | solution.py:71
  462.0 9.8 %custom-call.26 = f32[1,128,128]{1,2,0:T(8,128)S(1)} custom-call(f32[1,128,128]{2,1,0:T(8,128)S(1)} %get-tuple-element.62), custom_call_target="InvertDiagBlocksLowerTriangular" | custom-call | tf_op jit(solution)/shard_map/jit(cholesky)/cholesky | solution.py:71
  472.3 11.7 %cholesky.128 = f32[128,128]{1,0:T(8,128)S(1)} custom-call(f32[128,128]{1,0:T(8,128)S(1)} %convolution_subtract_fusion.3), custom_call_target="Cholesky" | custom-call | tf_op jit(solution)/shard_map/jit(cholesky)/cholesky | solution.py:71
  486.7 4.4 while.5
  487.7 1.4 bitcast_dynamic-update-slice_fusion.2
  489.7 1.4 bitcast_dynamic-update-slice_fusion.2
  491.1 19.7 %custom-call.33 = f32[2,128,128]{1,2,0:T(8,128)S(1)} custom-call(f32[2,128,128]{2,1,0:T(8,128)S(1)} %get-tuple-element.29), custom_call_target="InvertDiagBlocksLowerTriangular" | custom-call | tf_op jit(solution)/shard_map/triangular_solve/custom-call.5 | solution.py:20
  511.4 6.1 fusion.141
  517.5 2.5 stack.5
  520.0 9.5 %all-to-all-start.1 = ((f32[32,32,1024]{2,1,0:T(8,128)}), f32[32,32,1024]{2,1,0:T(8,128)}, u32[]{:S(2)}, u32[]{:S(2)}) async-start(f32[32,32,1024]{2,1,0:T(8,128)} %stack.5), calls=%async_computation.1 | async-start | bytes 8388608 | tf_op jit(solution)/shard_map/all_to_all | solution.py:81
  529.6 60.2 %all-gather.12.cloned.1.call-done = f32[1024,1024]{1,0:T(8,128)} async-done(((f32[32,1024]{1,0:T(8,128)}), f32[1024,1024]{1,0:T(8,128)}) %all-gather.12.cloned.1.call-update) | async-done | bytes 4194320 | tf_op jit(solution)/shard_map/all_gather | solution.py:132
  589.7 5.6 fusion.140
  597.5 0.7 fusion.60
  598.9 44.2 %all-gather.16.cloned.1.call-done = f32[1024,256]{1,0:T(8,128)} async-done(((f32[32,256]{1,0:T(8,128)}), f32[1024,256]{1,0:T(8,128)}) %all-gather.16.cloned.1.call-update) | async-done | bytes 1048592 | tf_op jit(solution)/shard_map/all_gather | solution.py:67
  643.1 9.2 %fusion.139 = f32[256,1024]{1,0:T(8,128)S(1)} fusion(f32[1024,256]{1,0:T(8,128)} %all-gather.16.cloned.1.call-done, f32[1024,1024]{1,0:T(8,128)} %all-gather.10.cloned.1.call-done), kind=kOutput, calls=%fused_computation.203 | convolution fusion | flops 3221225472 | bytes 6291456 | tf_op jit(solution)/shard_map/dot_general | solution.py:16
  654.3 0.7 fusion.24
  655.0 0.7 fusion.23
  655.8 4.1 fusion.14
  660.0 1.7 fusion.20
  661.7 5.4 fusion.11
  (125 shorter events, 19.4 us)
Async XLA Ops:
  7.2 57.8 %all-gather.8.cloned.1.call-start = ((), (), s32[]{:S(2)}) async-start(), calls=%async_computation.2 | async-start | bytes 3244032 | tf_op jit(solution)/shard_map/all_gather | solution.py:107
  68.6 7.2 %copy-start.9 = (f32[2,32,1024]{2,1,0:T(8,128)S(1)}, f32[2,32,1024]{2,1,0:T(8,128)}, u32[]{:S(2)}) copy-start(f32[2,32,1024]{2,1,0:T(8,128)} %param.14) | copy-start | bytes 786436
  73.9 2.0 copy-start
  82.7 6.8 %copy-start.10 = (f32[1,128,256]{2,1,0:T(8,128)S(1)}, f32[1,128,256]{2,1,0:T(8,128)}, u32[]{:S(2)}) copy-start(f32[1,128,256]{2,1,0:T(8,128)} %get-tuple-element.57) | copy-start | bytes 393220
  82.7 236.9 %all-to-all-start = ((f32[32,32,1024]{2,1,0:T(8,128)}), f32[32,32,1024]{2,1,0:T(8,128)}, u32[]{:S(2)}, u32[]{:S(2)}) async-start(f32[32,32,1024]{2,1,0:T(8,128)} %stack.4), calls=%async_computation | async-start | bytes 8388608 | tf_op jit(solution)/shard_map/all_to_all | solution.py:81
  88.1 133.3 %all-reduce.5.cloned.1.call-start = ((), (), s32[]{:S(2)}) async-start(), calls=%async_computation.3 | async-start | bytes 131072 | tf_op jit(solution)/shard_map/psum | solution.py:70
  89.1 235.7 %all-gather.14.cloned.1.call-start = ((), (), s32[]{:S(2)}) async-start(), calls=%async_computation.6 | async-start | bytes 1081344 | tf_op jit(solution)/shard_map/all_gather | solution.py:134
  251.9 1.9 copy-start.2
  257.6 4.7 collective-permute-start.1
  262.3 0.6 copy-start.13
  262.9 185.2 %all-reduce.7.cloned.1.call-start = ((), (), s32[]{:S(2)}) async-start(), calls=%async_computation.7 | async-start | bytes 524288 | tf_op jit(solution)/shard_map/psum | solution.py:70
  305.5 3.5 copy-start.1
  309.0 5.9 copy-start.6
  309.0 5.9 copy-start.3
  317.9 11.5 %copy-start.7 = (f32[32,1024]{1,0:T(8,128)}, f32[32,1024]{1,0:T(8,128)S(1)}, u32[]{:S(2)}) copy-start(f32[32,1024]{1,0:T(8,128)S(1)} %fusion.6) | copy-start | bytes 393220
  317.9 12.1 %copy-start.14 = (f32[2,32]{1,0:T(2,128)S(1)}, f32[2,32]{1,0:T(2,128)}, u32[]{:S(2)}) copy-start(f32[2,32]{1,0:T(2,128)} %param.13) | copy-start | bytes 772
  317.9 52.0 %copy-start.15 = (f32[2,32]{1,0:T(2,128)S(1)}, f32[2,32]{1,0:T(2,128)}, u32[]{:S(2)}) copy-start(f32[2,32]{1,0:T(2,128)} %param.17) | copy-start | bytes 772
  317.9 57.3 %copy-start.16 = (u32[256]{0:T(256)S(1)}, u32[256]{0:T(256)}, u32[]{:S(2)}) copy-start(u32[256]{0:T(256)} %constant.217) | copy-start | bytes 3076
  317.9 10.7 %collective-permute-start = (f32[32,1024]{1,0:T(8,128)S(1)}, f32[32,1024]{1,0:T(8,128)S(1)}, u32[]{:S(2)}, u32[]{:S(2)}) collective-permute-start(f32[32,1024]{1,0:T(8,128)S(1)} %fusion.6), channel_id=1, source_target_pairs={{32,0},{64,32},{96,64},{128,96},{160,128},{192,160},{224,192},{33,... | collective-permute-start | bytes 393224 | tf_op jit(solution)/shard_map/ppermute | solution.py:12
  326.6 121.4 %copy-start.11 = (f32[32,256]{1,0:T(8,128)}, f32[32,256]{1,0:T(8,128)S(1)}, u32[]{:S(2)}) copy-start(f32[32,256]{1,0:T(8,128)S(1)} %fusion.138) | copy-start | bytes 98308
  328.6 182.8 %all-gather.10.cloned.1.call-start = ((), (), s32[]{:S(2)}) async-start(), calls=%async_computation.4 | async-start | bytes 4325376 | tf_op jit(solution)/shard_map/all_gather | solution.py:133
  328.6 0.7 copy-start.12
  329.3 260.4 %all-gather.12.cloned.1.call-start = ((), (), s32[]{:S(2)}) async-start(), calls=%async_computation.5 | async-start | bytes 4325376 | tf_op jit(solution)/shard_map/all_gather | solution.py:132
  329.9 313.2 %all-gather.16.cloned.1.call-start = ((), (), s32[]{:S(2)}) async-start(), calls=%async_computation.8 | async-start | bytes 1081344 | tf_op jit(solution)/shard_map/all_gather | solution.py:67
  377.2 69.2 %collective-permute-start.2 = (f32[256]{0:T(256)S(1)}, f32[256]{0:T(256)S(1)}, u32[]{:S(2)}, u32[]{:S(2)}) collective-permute-start(f32[256]{0:T(256)S(1)} %pad_maximum_fusion.5), channel_id=1, source_target_pairs={{32,0},{64,32},{96,64},{128,96},{160,128},{192,160},{224,192},{33,... | collective-permute-start | bytes 3080 | tf_op jit(solution)/shard_map/ppermute | solution.py:12
  379.9 280.1 %collective-permute-start.3 = (f32[32]{0:T(128)S(1)}, f32[32]{0:T(128)S(1)}, u32[]{:S(2)}, u32[]{:S(2)}) collective-permute-start(f32[32]{0:T(128)S(1)} %fusion.16), channel_id=1, source_target_pairs={{32,0},{64,32},{96,64},{128,96},{160,128},{192,160},{224,192},{33,... | collective-permute-start | bytes 392 | tf_op jit(solution)/shard_map/ppermute | solution.py:12
  446.4 215.3 %collective-permute-start.4 = (f32[32,1024]{1,0:T(8,128)S(1)}, f32[32,1024]{1,0:T(8,128)S(1)}, u32[]{:S(2)}, u32[]{:S(2)}) collective-permute-start(f32[32,1024]{1,0:T(8,128)S(1)} %fusion.12), channel_id=1, source_target_pairs={{32,0},{64,32},{96,64},{128,96},{160,128},{192,160},{224,192},{33,... | collective-permute-start | bytes 393224 | tf_op jit(solution)/shard_map/ppermute | solution.py:12
  520.0 69.8 %copy-start.5 = (f32[1024,256]{1,0:T(8,128)S(1)}, f32[1024,256]{1,0:T(8,128)}, u32[]{:S(2)}) copy-start(f32[1024,256]{1,0:T(8,128)} %all-gather.14.cloned.1.call-done) | copy-start | bytes 3145732
  520.0 141.7 %all-to-all-start.1 = ((f32[32,32,1024]{2,1,0:T(8,128)}), f32[32,32,1024]{2,1,0:T(8,128)}, u32[]{:S(2)}, u32[]{:S(2)}) async-start(f32[32,32,1024]{2,1,0:T(8,128)} %stack.5), calls=%async_computation.1 | async-start | bytes 8388608 | tf_op jit(solution)/shard_map/all_to_all | solution.py:81
  652.3 3.5 copy-start.4
  652.3 3.5 copy-start.8
Sparse Core Ops, SparseCore 0:
  10.6 54.2 all-gather.7
  92.8 128.6 all-reduce.4
  263.0 48.0 all-gather.13
  328.7 113.9 all-reduce.6
  445.6 51.8 all-gather.9
  500.5 89.1 all-gather.11
  592.3 50.7 all-gather.15
